TPU v7x, 512 devices: a whole 4x4x16 slice. The times are simulated.
512 devices in a mesh: tm: 32 (over x, z_lo), height: 8 (over z_hi, y), dp: 2 (over core).
Axes of the slice: x: 4, y: 4, z: 16 (z_hi: 2, z_lo: 8; z = z_hi * 8 + z_lo), core: 2. Of those that a mesh axis runs over, the one named last changes fastest.
Arguments:
- frames_in: bfloat16 [2, 128, 32, 48, 256], P('dp', 'tm', 'height'), may hold values from -6 to 6
- cotangent: bfloat16 [2, 128, 32, 48, 256], P('dp', 'tm', 'height'), may hold values from -6 to 6
- w_spatial: bfloat16 [3, 3, 256, 256], replicated, may hold values from -0.125 to 0.125
- w_temporal: bfloat16 [3, 256, 256], replicated, may hold values from -0.21875 to 0.21875
Outputs:
- decoded: bfloat16 [2, 128, 32, 48, 256], P('dp', 'tm', 'height')
- input_grad: bfloat16 [2, 128, 32, 48, 256], P('dp', 'tm', 'height')
- spatial_grad: bfloat16 [3, 3, 256, 256], replicated
- temporal_grad: bfloat16 [3, 256, 256], replicated
All inputs are finite; a program needn't handle non-finite values.
Results may differ from a plain program's by a relative error of at most 0.0061.
Values may be sent and summed in bfloat16 or wider, within the bound.
No kernel may reach another device: no remote copies, remote signals or barrier semaphores. Data moves between devices by JAX's collectives and lax.ppermute only.
A program may use at most 64 MiB of HBM per device.

v0:
```python
import math
import jax
import jax.numpy as jnp
from jax import lax
from jax.sharding import PartitionSpec as P


def extended(x, sides, width):
    for axis, dim in sides:
        count, length = (lax.axis_size(axis), x.shape[dim])
        up = [(i, (i + 1) % count) for i in range(count - 1)]
        down = [(j, i) for i, j in up]
        last = lax.slice_in_dim(x, length - width, length, axis=dim)
        initial = lax.slice_in_dim(x, 0, width, axis=dim)
        before = lax.ppermute(last, axis, up)
        after = lax.ppermute(initial, axis, down)
        x = jnp.concatenate([before, x, after], axis=dim)
    return x


def from_behind(block, axis, distance):
    devices = range(lax.axis_size(axis))
    route = [(i - distance, i) for i in devices if i - distance in devices]
    return lax.ppermute(block, axis, route)


def silu_slope(values):
    sigmoid_value = jax.nn.sigmoid(values)
    return sigmoid_value * (1.0 + values * (1.0 - sigmoid_value))


def forward_taps(padded, row_count, col_count):
    pieces = [
        padded[:, row_tap : row_tap + row_count, col_tap : col_tap + col_count]
        for row_tap in range(3)
        for col_tap in range(3)
    ]
    return jnp.concatenate(pieces, axis=-1)


def backward_taps(padded, row_count, col_count):
    pieces = [
        padded[:, 2 - row_tap : 2 - row_tap + row_count, 2 - col_tap : 2 - col_tap + col_count]
        for row_tap in range(3)
        for col_tap in range(3)
    ]
    return jnp.concatenate(pieces, axis=-1)


def frame_taps(source, frame_count):
    return jnp.concatenate(
        [source[shift_tap : shift_tap + frame_count] for shift_tap in range(3)], axis=-1
    )


def flat_dot(left_side, right_side):
    return jnp.dot(
        left_side.reshape(-1, left_side.shape[-1]), right_side, preferred_element_type=jnp.float32
    )


def local(frames_in, cotangent, w_spatial, w_temporal):
    inputs = frames_in[0]
    upstream = cotangent[0]
    frame_count, row_count, col_count, channels = inputs.shape
    spatial_flat = w_spatial.reshape(9 * channels, channels)
    temporal_flat = w_temporal.reshape(3 * channels, channels)
    spatial_back = jnp.concatenate(
        [w_spatial[row_tap, col_tap].T for row_tap in range(3) for col_tap in range(3)], axis=0
    )
    temporal_back = jnp.concatenate([w_temporal[2].T, w_temporal[1].T, w_temporal[0].T], axis=0)
    first_shard = lax.axis_index("tm") == 0
    inputs_prev = from_behind(inputs[frame_count - 2 :], "tm", 1)
    upstream_next = from_behind(upstream[:2], "tm", -1)
    local_both = extended(jnp.concatenate([inputs, upstream], axis=-1), (("height", 1),), 1)
    rim_both = extended(jnp.concatenate([inputs_prev, upstream_next], axis=-1), (("height", 1),), 1)

    def spatial_forward(block):
        activ = jax.nn.silu(block.astype(jnp.float32)).astype(jnp.bfloat16)
        taps = forward_taps(jnp.pad(activ, ((0, 0), (0, 0), (1, 1), (0, 0))), row_count, col_count)
        out = flat_dot(taps, spatial_flat).astype(jnp.bfloat16)
        return (taps, out.reshape(block.shape[0], row_count, col_count, channels))

    activ_taps, spatial_out = spatial_forward(local_both[..., :channels])
    unused, spatial_rim = spatial_forward(rim_both[..., :channels])
    repeated = jnp.broadcast_to(spatial_out[:1], (2,) + spatial_out.shape[1:])
    earlier = jnp.where(first_shard, repeated, spatial_rim)
    padded_frames = jnp.concatenate([earlier, spatial_out], axis=0)
    frame_stack = frame_taps(padded_frames, frame_count).reshape(-1, 3 * channels)
    temporal_out = jnp.dot(frame_stack, temporal_flat, preferred_element_type=jnp.float32).reshape(
        inputs.shape
    )
    decoded = (inputs.astype(jnp.float32) + temporal_out).astype(jnp.bfloat16)

    def frame_gradient(source):
        rows = source.shape[1]
        part = flat_dot(frame_taps(source, frame_count), temporal_back)
        first_up = source[0].reshape(-1, channels)
        second_up = source[1].reshape(-1, channels)
        fold = jnp.dot(first_up, w_temporal[0].T, preferred_element_type=jnp.float32)
        fold = fold + jnp.dot(first_up, w_temporal[1].T, preferred_element_type=jnp.float32)
        fold = fold + jnp.dot(second_up, w_temporal[0].T, preferred_element_type=jnp.float32)
        part = part.reshape(frame_count, rows * col_count, channels)
        part = part.at[0].add(jnp.where(first_shard, fold, 0.0))
        return part.astype(jnp.bfloat16).reshape(frame_count, rows, col_count, channels)

    frame_grad = frame_gradient(jnp.concatenate([upstream, upstream_next], axis=0))
    up_rows = jnp.concatenate([local_both[..., channels:], rim_both[..., channels:]], axis=0)
    edge_grad = frame_gradient(jnp.stack([up_rows[:, 0], up_rows[:, row_count + 1]], axis=1))
    frame_grad_full = jnp.concatenate([edge_grad[:, :1], frame_grad, edge_grad[:, 1:]], axis=1)
    grad_pad = jnp.pad(frame_grad_full, ((0, 0), (0, 0), (1, 1), (0, 0)))
    act_grad = flat_dot(backward_taps(grad_pad, row_count, col_count), spatial_back)
    act_grad = act_grad.reshape(inputs.shape)
    input_grad = (
        upstream.astype(jnp.float32) + silu_slope(inputs.astype(jnp.float32)) * act_grad
    ).astype(jnp.bfloat16)
    cell_count = (
        frame_count
        * lax.axis_size("tm")
        * row_count
        * lax.axis_size("height")
        * col_count
        * lax.axis_size("dp")
    )
    grad_scale = 1.0 / math.sqrt(cell_count)
    contract = (((0,), (0,)), ((), ()))
    local_taps = activ_taps.reshape(-1, 9 * channels)
    spatial_term = lax.dot_general(
        local_taps, frame_grad.reshape(-1, channels), contract, preferred_element_type=jnp.float32
    )
    temporal_term = lax.dot_general(
        frame_stack, upstream.reshape(-1, channels), contract, preferred_element_type=jnp.float32
    )
    spatial_sum, temporal_sum = lax.psum(
        (spatial_term * grad_scale, temporal_term * grad_scale), ("tm", "height", "dp")
    )
    spatial_grad = spatial_sum.astype(jnp.bfloat16).reshape(3, 3, channels, channels)
    temporal_grad = temporal_sum.astype(jnp.bfloat16).reshape(3, channels, channels)
    return (decoded[None], input_grad[None], spatial_grad, temporal_grad)


def solution(mesh):
    return jax.shard_map(
        local,
        mesh=mesh,
        in_specs=(
            P("dp", "tm", "height", None, None),
            P("dp", "tm", "height", None, None),
            P(),
            P(),
        ),
        out_specs=(
            P("dp", "tm", "height", None, None),
            P("dp", "tm", "height", None, None),
            P(),
            P(),
        ),
        check_vma=False,
    )
```

profile of v0, /device:TPU:2, one launch (start us, length us, event | category | flops | bytes accessed | tf_op | source)
XLA Modules:
  0.0 259.6 jit_solution(6937136790871638325)
XLA Ops:
  0.7 1.7 slice_bitcast_fusion
  2.3 13.1 %collective-permute-start.3 = (bf16[2,4,48,256]{3,2,1,0:T(8,128)(2,1)}, bf16[2,4,48,256]{3,2,1,0:T(8,128)(2,1)S(1)}, u32[]{:S(2)}, u32[]{:S(2)}) collective-permute-start(bf16[2,4,48,256]{3,2,1,0:T(8,128)(2,1)} %slice_bitcast_fusion), channel_id=1, source_target_pairs={{16,0},{32,16},{48,32},{64,48},{80,64},{96,80},{112,96},{128,112},... | collective-permute-start | bytes 589832 | tf_op jit(solution)/shard_map/ppermute | solution.py:24
  15.5 1.6 slice_bitcast_fusion.1
  17.1 2.0 collective-permute-start.2
  19.1 1.8 pad_maximum_fusion.8
  20.9 3.5 %collective-permute-start = (bf16[4,1,48,512]{3,2,1,0:T(8,128)(2,1)}, bf16[4,1,48,512]{3,2,1,0:T(8,128)(2,1)S(1)}, u32[]{:S(2)}, u32[]{:S(2)}) collective-permute-start(bf16[4,1,48,512]{3,2,1,0:T(8,128)(2,1)} %get-tuple-element.39), channel_id=1, source_target_pairs={{0,2},{2,4},{4,6},{6,8},{8,10},{10,12},{12,14},{1,3},{3,5},{5,7},{... | collective-permute-start | bytes 589832 | tf_op jit(solution)/shard_map/ppermute | solution.py:15
  24.4 1.3 collective-permute-start.1
  25.8 0.2 fusion.75
  26.0 0.2 convolution_add_fusion.2
  26.3 0.1 copy.33
  27.4 1.0 copy-done.12
  28.8 4.5 %collective-permute-done.2 = bf16[2,4,48,256]{3,2,1,0:T(8,128)(2,1)} collective-permute-done((bf16[2,4,48,256]{3,2,1,0:T(8,128)(2,1)}, bf16[2,4,48,256]{3,2,1,0:T(8,128)(2,1)}, u32[]{:S(2)}, u32[]{:S(2)}) %collective-permute-start.2) | collective-permute-done | bytes 196640 | tf_op jit(solution)/shard_map/ppermute | solution.py:24
  33.3 0.9 constant_dynamic-update-slice_fusion.1
  34.3 3.5 %collective-permute-start.4 = (bf16[2,1,48,512]{3,2,1,0:T(8,128)(2,1)S(1)}, bf16[2,1,48,512]{3,2,1,0:T(8,128)(2,1)S(1)}, u32[]{:S(2)}, u32[]{:S(2)}) collective-permute-start(bf16[2,1,48,512]{3,2,1,0:T(8,128)(2,1)S(1)} %get-tuple-element.50), channel_id=1, source_target_pairs={{0,2},{2,4},{4,6},{6,8},{8,10},{10,12},{12,14},{1,3},{3,5},{5,7},{... | collective-permute-start | bytes 294920 | tf_op jit(solution)/shard_map/ppermute | solution.py:15
  37.8 1.3 collective-permute-start.5
  39.1 0.5 fusion.15
  39.7 0.2 fusion.71
  40.0 0.7 copy-done.3
  40.6 1.0 pad_maximum_fusion
  41.7 0.4 fusion.9
  42.1 0.1 fusion.51
  42.2 0.1 fusion.52
  42.3 0.1 fusion.53
  42.5 0.1 fusion.54
  42.6 0.1 fusion.55
  42.8 0.1 fusion.56
  42.9 1.1 convolution_multiply_fusion
  44.1 0.1 copy-done.5
  44.2 1.1 convolution_convert_fusion
  45.4 0.2 fusion.46
  45.6 0.4 copy-done.6
  46.0 0.5 slice-done
  46.6 0.2 fusion.78
  46.8 0.2 convolution_add_fusion.4
  47.0 0.4 copy-done.9
  47.5 0.3 fusion.64
  47.8 0.2 fusion.32
  48.5 0.6 convolution_convert_fusion.1
  49.1 0.3 fusion.42
  49.4 0.1 slice_dynamic-update-slice_fusion.5
  49.6 0.1 slice_dynamic-update-slice_fusion.3
  49.8 0.1 slice_dynamic-update-slice_fusion.1
  50.0 0.6 slice-done.1
  50.7 0.2 copy-done.7
  50.9 1.2 fusion.4
  52.2 1.4 convolution_multiply_fusion.1
  53.5 1.9 fusion.5
  55.5 204.1 %all-reduce.5 = (bf16[2304,256]{1,0:T(8,128)(2,1)}, bf16[768,256]{1,0:T(8,128)(2,1)}) all-reduce(f32[2304,256]{1,0:T(8,128)S(1)} %convolution_multiply_fusion, f32[768,256]{1,0:T(8,128)} %convolution_multiply_fusion.1), channel_id=1, replica_groups=mesh['tm'=32,'height'=8,'dp'=2] {'tm','height','dp'}, use_global_device_ids=true, to_apply=%region_0.1 | all-reduce | flops 786432 | bytes 4718592 | tf_op jit(solution)/shard_map/psum | solution.py:134
  (84 shorter events, 2.5 us)
Async XLA Ops:
  0.6 25.1 %copy-start = (bf16[1,4,4,48,256]{4,3,2,1,0:T(8,128)(2,1)S(1)}, bf16[1,4,4,48,256]{4,3,2,1,0:T(8,128)(2,1)}, u32[]{:S(2)}) copy-start(bf16[1,4,4,48,256]{4,3,2,1,0:T(8,128)(2,1)} %param.9) | copy-start | bytes 1179652
  0.6 25.1 %copy-start.2 = (bf16[3,256,256]{2,1,0:T(8,128)(2,1)S(1)}, bf16[3,256,256]{2,1,0:T(8,128)(2,1)}, u32[]{:S(2)}) copy-start(bf16[3,256,256]{2,1,0:T(8,128)(2,1)} %param.11) | copy-start | bytes 1179652
  2.3 31.9 %collective-permute-start.3 = (bf16[2,4,48,256]{3,2,1,0:T(8,128)(2,1)}, bf16[2,4,48,256]{3,2,1,0:T(8,128)(2,1)S(1)}, u32[]{:S(2)}, u32[]{:S(2)}) collective-permute-start(bf16[2,4,48,256]{3,2,1,0:T(8,128)(2,1)} %slice_bitcast_fusion), channel_id=1, source_target_pairs={{16,0},{32,16},{48,32},{64,48},{80,64},{96,80},{112,96},{128,112},... | collective-permute-start | bytes 589832 | tf_op jit(solution)/shard_map/ppermute | solution.py:24
  17.1 9.1 %copy-start.4 = (bf16[3,3,256,256]{3,2,1,0:T(8,128)(2,1)S(1)}, bf16[3,3,256,256]{3,2,1,0:T(8,128)(2,1)}, u32[]{:S(2)}) copy-start(bf16[3,3,256,256]{3,2,1,0:T(8,128)(2,1)} %param.10) | copy-start | bytes 3538948
  17.1 16.2 %collective-permute-start.2 = (bf16[2,4,48,256]{3,2,1,0:T(8,128)(2,1)}, bf16[2,4,48,256]{3,2,1,0:T(8,128)(2,1)}, u32[]{:S(2)}, u32[]{:S(2)}) collective-permute-start(bf16[2,4,48,256]{3,2,1,0:T(8,128)(2,1)} %slice_bitcast_fusion.1), channel_id=1, source_target_pairs={{0,16},{16,32},{32,48},{48,64},{64,80},{80,96},{96,112},{112,128},... | collective-permute-start | bytes 589832 | tf_op jit(solution)/shard_map/ppermute | solution.py:24
  20.9 19.1 %collective-permute-start = (bf16[4,1,48,512]{3,2,1,0:T(8,128)(2,1)}, bf16[4,1,48,512]{3,2,1,0:T(8,128)(2,1)S(1)}, u32[]{:S(2)}, u32[]{:S(2)}) collective-permute-start(bf16[4,1,48,512]{3,2,1,0:T(8,128)(2,1)} %get-tuple-element.39), channel_id=1, source_target_pairs={{0,2},{2,4},{4,6},{6,8},{8,10},{10,12},{12,14},{1,3},{3,5},{5,7},{... | collective-permute-start | bytes 589832 | tf_op jit(solution)/shard_map/ppermute | solution.py:15
  24.4 15.6 %collective-permute-start.1 = (bf16[4,1,48,512]{3,2,1,0:T(8,128)(2,1)S(1)}, bf16[4,1,48,512]{3,2,1,0:T(8,128)(2,1)}, u32[]{:S(2)}, u32[]{:S(2)}) collective-permute-start(bf16[4,1,48,512]{3,2,1,0:T(8,128)(2,1)S(1)} %get-tuple-element.40), channel_id=1, source_target_pairs={{2,0},{4,2},{6,4},{8,6},{10,8},{12,10},{14,12},{3,1},{5,3},{7,5},{... | collective-permute-start | bytes 589832 | tf_op jit(solution)/shard_map/ppermute | solution.py:16
  27.4 1.0 copy-start.12
  28.6 11.0 %copy-start.8 = (bf16[1,256,256]{1,2,0:T(8,128)(2,1)}, bf16[1,256,256]{1,2,0:T(8,128)(2,1)S(1)}, u32[]{:S(2)}) copy-start(bf16[1,256,256]{1,2,0:T(8,128)(2,1)S(1)} %copy.23) | copy-start | bytes 393220
  28.8 10.9 %copy-start.10 = (bf16[1,256,256]{1,2,0:T(8,128)(2,1)}, bf16[1,256,256]{1,2,0:T(8,128)(2,1)S(1)}, u32[]{:S(2)}) copy-start(bf16[1,256,256]{1,2,0:T(8,128)(2,1)S(1)} %copy.24) | copy-start | bytes 393220
  34.3 11.0 %collective-permute-start.4 = (bf16[2,1,48,512]{3,2,1,0:T(8,128)(2,1)S(1)}, bf16[2,1,48,512]{3,2,1,0:T(8,128)(2,1)S(1)}, u32[]{:S(2)}, u32[]{:S(2)}) collective-permute-start(bf16[2,1,48,512]{3,2,1,0:T(8,128)(2,1)S(1)} %get-tuple-element.50), channel_id=1, source_target_pairs={{0,2},{2,4},{4,6},{6,8},{8,10},{10,12},{12,14},{1,3},{3,5},{5,7},{... | collective-permute-start | bytes 294920 | tf_op jit(solution)/shard_map/ppermute | solution.py:15
  37.8 7.5 %collective-permute-start.5 = (bf16[2,1,48,512]{3,2,1,0:T(8,128)(2,1)S(1)}, bf16[2,1,48,512]{3,2,1,0:T(8,128)(2,1)S(1)}, u32[]{:S(2)}, u32[]{:S(2)}) collective-permute-start(bf16[2,1,48,512]{3,2,1,0:T(8,128)(2,1)S(1)} %get-tuple-element.51), channel_id=1, source_target_pairs={{2,0},{4,2},{6,4},{8,6},{10,8},{12,10},{14,12},{3,1},{5,3},{7,5},{... | collective-permute-start | bytes 294920 | tf_op jit(solution)/shard_map/ppermute | solution.py:16
  39.6 1.0 copy-start.3
  41.7 3.6 %copy-start.1 = (bf16[4,6,48,512]{3,2,1,0:T(8,128)(2,1)}, bf16[4,6,48,512]{3,2,1,0:T(8,128)(2,1)S(1)}, u32[]{:S(2)}) copy-start(bf16[4,6,48,512]{3,2,1,0:T(8,128)(2,1)S(1)} %pad_maximum_fusion) | copy-start | bytes 3538948
  42.9 1.3 copy-start.5
  45.3 0.7 copy-start.6
  45.3 1.2 slice-start
  46.5 0.9 copy-start.9
  46.5 1.0 copy-start.11
  49.8 0.9 slice-start.1
  49.8 1.1 copy-start.7
  52.2 1.4 copy-start.13
where the time goes:
time: 260 us
  blocking collectives  204 us (78%)
  starting transfers between devices  24.7 us (10%)
  local copies, waits for them, and re-layouts  11.3 us (4%)
  matrix products  9.46 us (4%)
  waiting for transfers between devices  4.52 us (2%)
  other arithmetic  4.02 us (2%)
    psum x1, blocking collectives, local(): lax.psum((spatial_term * grad_scale, temporal_term * grad_scale), ('tm',...  204 us
    ppermute x2, starting transfers between devices, from_behind(): return lax.ppermute(block, axis, route)  15.2 us
    ppermute x2, starting transfers between devices, extended(): before = lax.ppermute(last, axis, up)  6.97 us
    unnamed x71, local copies, waits for them, and re-layouts  6.45 us
  transfers between devices with their start and end apart: 6, of which 1 were waited for; matrix products, arithmetic and copies ran while one was open for 4% of the time, Pallas kernels for 0%

commit v1 on v0

--- a/solution.py
+++ b/solution.py
@@ -3,6 +3,11 @@
 import jax.numpy as jnp
 from jax import lax
 from jax.sharding import PartitionSpec as P
+
+
+def one_after_other(value, inner_axis, outer_axis):
+    inner = lax.psum(value, inner_axis)
+    return lax.psum(inner, outer_axis)
 
 
 def extended(x, sides, width):
@@ -131,8 +136,8 @@
     temporal_term = lax.dot_general(
         frame_stack, upstream.reshape(-1, channels), contract, preferred_element_type=jnp.float32
     )
-    spatial_sum, temporal_sum = lax.psum(
-        (spatial_term * grad_scale, temporal_term * grad_scale), ("tm", "height", "dp")
+    spatial_sum, temporal_sum = one_after_other(
+        (spatial_term * grad_scale, temporal_term * grad_scale), ("height", "dp"), "tm"
     )
     spatial_grad = spatial_sum.astype(jnp.bfloat16).reshape(3, 3, channels, channels)
     temporal_grad = temporal_sum.astype(jnp.bfloat16).reshape(3, channels, channels)

time: 260 us -> 672 us (2.58)
  the two profiles are of different devices: /device:TPU:2 before, /device:TPU:24 now
where the time goes in v1:
time: 672 us; the launch traced here: 671 us
  waiting for transfers between devices  295 us (44%)
  blocking collectives  281 us (42%)
  starting transfers between devices  40.6 us (6%)
  local copies, waits for them, and re-layouts  24.9 us (4%)
  between operations  14.8 us (2%)
  matrix products  10.9 us (2%)
    psum x1, waiting for transfers between devices, one_after_other(): inner = lax.psum(value, inner_axis)  287 us
    psum x1, blocking collectives, one_after_other(): return lax.psum(inner, outer_axis)  281 us
    ppermute x2, starting transfers between devices, extended(): before = lax.ppermute(last, axis, up)  30.1 us
    unnamed x85, local copies, waits for them, and re-layouts  18.8 us
  transfers between devices with their start and end apart: 7, of which 2 were waited for; matrix products, arithmetic and copies ran while one was open for 5% of the time, Pallas kernels for 0%

profile of v1, /device:TPU:24, one launch (start us, length us, event | category | flops | bytes accessed | tf_op | source)
XLA Modules:
  0.0 671.0 jit_solution(3658747555205661563)
XLA Ops:
  7.2 1.7 slice_bitcast_fusion
  8.9 1.3 collective-permute-start.3
  10.2 1.6 slice_bitcast_fusion.1
  11.8 5.4 collective-permute-start.2
  17.2 1.8 pad_maximum_fusion.8
  19.0 15.4 %collective-permute-start = (bf16[4,1,48,512]{3,2,1,0:T(8,128)(2,1)}, bf16[4,1,48,512]{3,2,1,0:T(8,128)(2,1)}, u32[]{:S(2)}, u32[]{:S(2)}) collective-permute-start(bf16[4,1,48,512]{3,2,1,0:T(8,128)(2,1)} %get-tuple-element.41), channel_id=1, source_target_pairs={{0,2},{2,4},{4,6},{6,8},{8,10},{10,12},{12,14},{1,3},{3,5},{5,7},{... | collective-permute-start | bytes 589832 | tf_op jit(solution)/shard_map/ppermute | solution.py:20
  34.4 1.9 collective-permute-start.1
  36.3 0.6 fusion.93
  36.9 0.8 fusion.94
  38.1 0.8 fusion.92
  38.9 1.7 copy.33
  40.6 1.7 copy.32
  42.2 0.8 copy.31
  43.0 0.8 copy.30
  43.8 0.8 copy.29
  44.5 0.7 copy.28
  45.3 0.7 copy.27
  46.3 0.9 bitcast_dynamic-update-slice_fusion.6
  47.2 0.9 bitcast_dynamic-update-slice_fusion.5
  48.1 0.9 bitcast_dynamic-update-slice_fusion.4
  49.1 1.1 copy-done.19
  50.2 1.0 copy.22
  51.2 1.0 copy.23
  52.3 1.0 copy.24
  53.4 1.0 constant_dynamic-update-slice_fusion.1
  54.4 14.8 %collective-permute-start.4 = (bf16[2,1,48,512]{3,2,1,0:T(8,128)(2,1)S(1)}, bf16[2,1,48,512]{3,2,1,0:T(8,128)(2,1)S(1)}, u32[]{:S(2)}, u32[]{:S(2)}) collective-permute-start(bf16[2,1,48,512]{3,2,1,0:T(8,128)(2,1)S(1)} %get-tuple-element.52), channel_id=1, source_target_pairs={{0,2},{2,4},{4,6},{6,8},{8,10},{10,12},{12,14},{1,3},{3,5},{5,7},{... | collective-permute-start | bytes 294920 | tf_op jit(solution)/shard_map/ppermute | solution.py:20
  69.2 1.9 collective-permute-start.5
  71.2 0.5 fusion.15
  71.7 0.4 copy-done.12
  72.0 0.2 fusion.71
  72.4 0.3 copy-done.3
  72.7 1.1 pad_maximum_fusion
  73.8 0.4 fusion.9
  75.0 2.6 convolution_multiply_fusion
  77.6 1.1 convolution_convert_fusion
  78.7 7.9 %collective-permute-done.5 = bf16[2,1,48,512]{3,2,1,0:T(8,128)(2,1)S(1)} collective-permute-done((bf16[2,1,48,512]{3,2,1,0:T(8,128)(2,1)S(1)}, bf16[2,1,48,512]{3,2,1,0:T(8,128)(2,1)S(1)}, u32[]{:S(2)}, u32[]{:S(2)}) %collective-permute-start.5) | collective-permute-done | bytes 98336 | tf_op jit(solution)/shard_map/ppermute | solution.py:21
  87.2 0.2 convolution_add_fusion.4
  87.5 0.4 copy-done.14
  88.0 0.3 fusion.64
  88.7 0.6 convolution_convert_fusion.1
  89.4 0.2 slice-done.1
  89.9 1.4 convolution_multiply_fusion.1
  91.5 0.3 fusion.42
  92.4 0.7 copy-done.7
  93.2 1.2 fusion.4
  94.5 1.9 fusion.5
  96.4 287.2 %all-reduce.8.cloned.1.call-done = (f32[2304,256]{1,0:T(8,128)}, f32[768,256]{1,0:T(8,128)}) async-done(((f32[2304,256]{1,0:T(8,128)}, f32[768,256]{1,0:T(8,128)}), (f32[2304,256]{1,0:T(8,128)}, f32[768,256]{1,0:T(8,128)})) %all-reduce.8.cloned.1.call-update) | async-done | bytes 3145744 | tf_op jit(solution)/shard_map/psum | solution.py:9
  383.6 280.6 %all-reduce.9 = (bf16[2304,256]{1,0:T(8,128)(2,1)}, bf16[768,256]{1,0:T(8,128)(2,1)}) all-reduce(f32[2304,256]{1,0:T(8,128)} %get-tuple-element.30, f32[768,256]{1,0:T(8,128)} %get-tuple-element.31), channel_id=1, replica_groups=mesh['tm'=32,'height'=8,'dp'=2] {'tm'}, use_global_device_ids=true, to_apply=%region_1.2 | all-reduce | flops 786432 | bytes 4718592 | tf_op jit(solution)/shard_map/psum | solution.py:10
  (101 shorter events, 3.8 us)
Async XLA Ops:
  7.2 29.1 %copy-start = (bf16[1,4,4,48,256]{4,3,2,1,0:T(8,128)(2,1)S(1)}, bf16[1,4,4,48,256]{4,3,2,1,0:T(8,128)(2,1)}, u32[]{:S(2)}) copy-start(bf16[1,4,4,48,256]{4,3,2,1,0:T(8,128)(2,1)} %param.9) | copy-start | bytes 1179652
  7.2 29.8 %copy-start.2 = (bf16[3,256,256]{2,1,0:T(8,128)(2,1)S(1)}, bf16[3,256,256]{2,1,0:T(8,128)(2,1)}, u32[]{:S(2)}) copy-start(bf16[3,256,256]{2,1,0:T(8,128)(2,1)} %param.11) | copy-start | bytes 1179652
  7.2 376.4 %all-reduce.8.cloned.1.call-start = ((), (), s32[]{:S(2)}) async-start(), calls=%async_computation | async-start | bytes 6291456 | tf_op jit(solution)/shard_map/psum | solution.py:9
  8.9 45.4 %collective-permute-start.3 = (bf16[2,4,48,256]{3,2,1,0:T(8,128)(2,1)}, bf16[2,4,48,256]{3,2,1,0:T(8,128)(2,1)S(1)}, u32[]{:S(2)}, u32[]{:S(2)}) collective-permute-start(bf16[2,4,48,256]{3,2,1,0:T(8,128)(2,1)} %slice_bitcast_fusion), channel_id=1, source_target_pairs={{16,0},{32,16},{48,32},{64,48},{80,64},{96,80},{112,96},{128,112},... | collective-permute-start | bytes 589832 | tf_op jit(solution)/shard_map/ppermute | solution.py:29
  11.8 26.3 %copy-start.4 = (bf16[3,3,256,256]{3,2,1,0:T(8,128)(2,1)S(1)}, bf16[3,3,256,256]{3,2,1,0:T(8,128)(2,1)}, u32[]{:S(2)}) copy-start(bf16[3,3,256,256]{3,2,1,0:T(8,128)(2,1)} %param.10) | copy-start | bytes 3538948
  11.8 41.5 %collective-permute-start.2 = (bf16[2,4,48,256]{3,2,1,0:T(8,128)(2,1)}, bf16[2,4,48,256]{3,2,1,0:T(8,128)(2,1)}, u32[]{:S(2)}, u32[]{:S(2)}) collective-permute-start(bf16[2,4,48,256]{3,2,1,0:T(8,128)(2,1)} %slice_bitcast_fusion.1), channel_id=1, source_target_pairs={{0,16},{16,32},{32,48},{48,64},{64,80},{80,96},{96,112},{112,128},... | collective-permute-start | bytes 589832 | tf_op jit(solution)/shard_map/ppermute | solution.py:29
  19.0 53.4 %collective-permute-start = (bf16[4,1,48,512]{3,2,1,0:T(8,128)(2,1)}, bf16[4,1,48,512]{3,2,1,0:T(8,128)(2,1)}, u32[]{:S(2)}, u32[]{:S(2)}) collective-permute-start(bf16[4,1,48,512]{3,2,1,0:T(8,128)(2,1)} %get-tuple-element.41), channel_id=1, source_target_pairs={{0,2},{2,4},{4,6},{6,8},{8,10},{10,12},{12,14},{1,3},{3,5},{5,7},{... | collective-permute-start | bytes 589832 | tf_op jit(solution)/shard_map/ppermute | solution.py:20
  34.4 38.0 %collective-permute-start.1 = (bf16[4,1,48,512]{3,2,1,0:T(8,128)(2,1)}, bf16[4,1,48,512]{3,2,1,0:T(8,128)(2,1)}, u32[]{:S(2)}, u32[]{:S(2)}) collective-permute-start(bf16[4,1,48,512]{3,2,1,0:T(8,128)(2,1)} %get-tuple-element.42), channel_id=1, source_target_pairs={{2,0},{4,2},{6,4},{8,6},{10,8},{12,10},{14,12},{3,1},{5,3},{7,5},{... | collective-permute-start | bytes 589832 | tf_op jit(solution)/shard_map/ppermute | solution.py:21
  43.0 6.1 copy-start.9
  43.8 5.4 copy-start.8
  44.5 4.5 copy-start.10
  45.3 3.8 copy-start.11
  49.1 1.1 copy-start.19
  51.2 20.4 %copy-start.13 = (bf16[1,256,256]{1,2,0:T(8,128)(2,1)}, bf16[1,256,256]{1,2,0:T(8,128)(2,1)S(1)}, u32[]{:S(2)}) copy-start(bf16[1,256,256]{1,2,0:T(8,128)(2,1)S(1)} %copy.22) | copy-start | bytes 393220
  52.3 19.4 %copy-start.15 = (bf16[1,256,256]{1,2,0:T(8,128)(2,1)}, bf16[1,256,256]{1,2,0:T(8,128)(2,1)S(1)}, u32[]{:S(2)}) copy-start(bf16[1,256,256]{1,2,0:T(8,128)(2,1)S(1)} %copy.23) | copy-start | bytes 393220
  53.3 18.3 %copy-start.17 = (bf16[1,256,256]{1,2,0:T(8,128)(2,1)}, bf16[1,256,256]{1,2,0:T(8,128)(2,1)S(1)}, u32[]{:S(2)}) copy-start(bf16[1,256,256]{1,2,0:T(8,128)(2,1)S(1)} %copy.24) | copy-start | bytes 393220
  54.4 24.3 %collective-permute-start.4 = (bf16[2,1,48,512]{3,2,1,0:T(8,128)(2,1)S(1)}, bf16[2,1,48,512]{3,2,1,0:T(8,128)(2,1)S(1)}, u32[]{:S(2)}, u32[]{:S(2)}) collective-permute-start(bf16[2,1,48,512]{3,2,1,0:T(8,128)(2,1)S(1)} %get-tuple-element.52), channel_id=1, source_target_pairs={{0,2},{2,4},{4,6},{6,8},{8,10},{10,12},{12,14},{1,3},{3,5},{5,7},{... | collective-permute-start | bytes 294920 | tf_op jit(solution)/shard_map/ppermute | solution.py:20
  69.2 17.4 %collective-permute-start.5 = (bf16[2,1,48,512]{3,2,1,0:T(8,128)(2,1)S(1)}, bf16[2,1,48,512]{3,2,1,0:T(8,128)(2,1)S(1)}, u32[]{:S(2)}, u32[]{:S(2)}) collective-permute-start(bf16[2,1,48,512]{3,2,1,0:T(8,128)(2,1)S(1)} %get-tuple-element.53), channel_id=1, source_target_pairs={{2,0},{4,2},{6,4},{8,6},{10,8},{12,10},{14,12},{3,1},{5,3},{7,5},{... | collective-permute-start | bytes 294920 | tf_op jit(solution)/shard_map/ppermute | solution.py:21
  71.2 0.9 copy-start.12
  71.7 1.0 copy-start.3
  73.8 4.9 copy-start.1
  78.7 8.2 %copy-start.5 = (bf16[768,256]{1,0:T(8,128)(2,1)}, bf16[768,256]{1,0:T(8,128)(2,1)S(1)}, u32[]{:S(2)}) copy-start(bf16[768,256]{1,0:T(8,128)(2,1)S(1)} %convolution_convert_fusion) | copy-start | bytes 1179652
  78.7 8.2 %slice-start = ((bf16[4,6,48,512]{3,2,1,0:T(8,128)(2,1)}), bf16[4,6,48,256]{3,2,1,0:T(8,128)(2,1)S(1)}, s32[]{:S(2)}) async-start(bf16[4,6,48,512]{3,2,1,0:T(8,128)(2,1)} %copy-done.1), calls=%async_computation.1 | async-start | bytes 1179648 | tf_op jit(solution)/shard_map/slice | solution.py:113
  86.9 0.9 copy-start.14
  87.0 1.0 copy-start.16
  87.0 1.0 copy-start.18
  88.7 0.9 slice-start.1
  88.7 1.1 copy-start.6
  92.2 1.0 copy-start.7
  93.2 1.3 copy-start.20
Sparse Core Ops, SparseCore 0:
  91.4 292.1 all-reduce.7
